TPU v7x, 32 devices: a whole 2x2x4 slice. The times are simulated.
32 devices in a mesh: replica: 16 (over z, x, core), shard: 2 (over y).
Axes of the slice: x: 2, y: 2, z: 4, core: 2. Of those that a mesh axis runs over, the one named last changes fastest.
Arguments:
- frames: bfloat16 [32768, 768], P(('replica', 'shard')), may hold values from -6 to 6
- cotangent: bfloat16 [32768, 768], P(('replica', 'shard')), may hold values from -6 to 6
- segment_ids: int32 [32, 1024], P(('replica', 'shard')), may hold values from 0 to 7, never falling along the last dimension, each value on 1 to 512 neighbouring positions
- norm_gain: bfloat16 [2, 768], P(None, 'shard'), may hold values from 0.099609375 to 1.8984375
- norm_bias: bfloat16 [2, 768], P(None, 'shard'), may hold values from -2 to 2
- w_qkv: bfloat16 [768, 2304], P('shard'), may hold values from -0.21875 to 0.21875
- qv_bias: bfloat16 [2, 768], P(None, 'shard'), may hold values from -2 to 2
- w_out: bfloat16 [768, 768], P('shard'), may hold values from -0.875 to 0.875
- out_bias: bfloat16 [2, 768], P(None, 'shard'), may hold values from -2 to 2
- w_up: bfloat16 [768, 3072], P(None, 'shard'), may hold values from -0.21875 to 0.21875
- up_bias: bfloat16 [3072], P('shard'), may hold values from -3 to 3
- w_down: bfloat16 [3072, 768], P('shard'), may hold values from -0.109375 to 0.109375
Outputs:
- out_frames: bfloat16 [32768, 768], P(('replica', 'shard'))
- d_frames: float32 [32768, 768], P(('replica', 'shard'))
- d_norm_gain: float32 [2, 768], P(None, 'shard')
- d_norm_bias: float32 [2, 768], P(None, 'shard')
- d_w_qkv: float32 [768, 2304], P('shard')
- d_qv_bias: float32 [2, 768], P(None, 'shard')
- d_w_out: float32 [768, 768], P('shard')
- d_out_bias: float32 [2, 768], P(None, 'shard')
- d_w_up: float32 [768, 3072], P(None, 'shard')
- d_up_bias: float32 [3072], P('shard')
- d_w_down: float32 [3072, 768], P('shard')
Inputs may be any that keep to these rules, and one draw needn't show every extreme that they name: `segment_ids`: each row numbers the documents of one sequence in order: never falling, every number of 0 to 7 used, no document longer than 512 frames, and one exactly that long in every row.
All inputs are finite; a program needn't handle non-finite values.
Results may differ from a plain program's by a relative error of at most 0.018.
Values may be sent and summed in bfloat16 or wider, within the bound.
No kernel may reach another device: no remote copies, remote signals or barrier semaphores. Data moves between devices by JAX's collectives and lax.ppermute only.
A program may use at most 256 MiB of HBM per device.

v0:
```python
import math
import jax
import jax.numpy as jnp
from jax import lax
from jax.sharding import PartitionSpec as P

H = 12
EPS = 1e-05
NEG = -1e30


def standardize(values):
    centered = values - jnp.mean(values, axis=1, keepdims=True)
    inverse = lax.rsqrt(jnp.mean(centered * centered, axis=1, keepdims=True) + EPS)
    return (centered * inverse, inverse)


def norm_back(grad_unit, unit, inverse):
    return inverse * (
        grad_unit
        - jnp.mean(grad_unit, axis=1, keepdims=True)
        - unit * jnp.mean(grad_unit * unit, axis=1, keepdims=True)
    )


def gelu_exact(values):
    return jax.nn.gelu(values, approximate=False)


def gelu_back(values, gradient):
    _, pull = jax.vjp(gelu_exact, values)
    return pull(gradient)[0]


def halves(array, which, axis):
    size = array.shape[axis] // 2
    return lax.slice_in_dim(array, which * size, (which + 1) * size, axis=axis)


def touching(query_seg, key_seg):
    return jnp.logical_and(query_seg[-1] >= key_seg[0], query_seg[0] <= key_seg[-1])


def keep_same(carry):
    return carry


def masked_scores(query_part, key_part, query_seg, key_seg):
    scale = 1.0 / math.sqrt(query_part.shape[2])
    raw = (
        jnp.einsum("qhd,khd->hqk", query_part, key_part, preferred_element_type=jnp.float32) * scale
    )
    same = query_seg[:, None] == key_seg[None, :]
    return jnp.where(same[None], raw, NEG)


def attend_forward(packed):
    queries, key_rows, value_rows, segment = packed
    outputs = []
    norms = []
    for query_pos in range(2):
        query_part = halves(queries, query_pos, 0)
        query_seg = halves(segment, query_pos, 0)
        span, heads, head_dim = query_part.shape
        peak = jnp.full((heads, span), NEG, jnp.float32)
        mass = jnp.zeros((heads, span), jnp.float32)
        for key_pos in range(2):
            key_part = halves(key_rows, key_pos, 0)
            key_seg = halves(segment, key_pos, 0)

            def grow(
                carry,
                key_part=key_part,
                key_seg=key_seg,
                query_part=query_part,
                query_seg=query_seg,
            ):
                old_peak, old_mass = carry
                scores = masked_scores(query_part, key_part, query_seg, key_seg)
                new_peak = jnp.maximum(old_peak, jnp.max(scores, axis=2))
                new_mass = old_mass * jnp.exp(old_peak - new_peak) + jnp.sum(
                    jnp.exp(scores - new_peak[:, :, None]), axis=2
                )
                return (new_peak, new_mass)

            peak, mass = lax.cond(touching(query_seg, key_seg), grow, keep_same, (peak, mass))
        log_norm = peak + jnp.log(mass)
        running = jnp.zeros((span, heads, head_dim), jnp.float32)
        for key_pos in range(2):
            key_part = halves(key_rows, key_pos, 0)
            value_part = halves(value_rows, key_pos, 0)
            key_seg = halves(segment, key_pos, 0)

            def spread(
                carry,
                key_part=key_part,
                value_part=value_part,
                key_seg=key_seg,
                query_part=query_part,
                query_seg=query_seg,
                log_norm=log_norm,
            ):
                scores = masked_scores(query_part, key_part, query_seg, key_seg)
                weights = jnp.exp(scores - log_norm[:, :, None]).astype(jnp.bfloat16)
                return carry + jnp.einsum(
                    "hqk,khd->qhd", weights, value_part, preferred_element_type=jnp.float32
                )

            running = lax.cond(touching(query_seg, key_seg), spread, keep_same, running)
        outputs.append(running)
        norms.append(log_norm)
    return (jnp.concatenate(outputs, axis=0), jnp.concatenate(norms, axis=1))


def attend_backward(packed):
    queries, key_rows, value_rows, segment, log_norm, grad_mixed, attended = packed
    scale = 1.0 / math.sqrt(queries.shape[2])
    row_dot = jnp.sum(grad_mixed * attended, axis=2).T
    query_grads = [jnp.zeros(halves(queries, 0, 0).shape, jnp.float32) for which in range(2)]
    key_grads = [jnp.zeros(halves(queries, 0, 0).shape, jnp.float32) for which in range(2)]
    value_grads = [jnp.zeros(halves(queries, 0, 0).shape, jnp.float32) for which in range(2)]
    for query_pos in range(2):
        query_part = halves(queries, query_pos, 0)
        query_seg = halves(segment, query_pos, 0)
        grad_part = halves(grad_mixed, query_pos, 0)
        norm_part = halves(log_norm, query_pos, 1)
        dot_part = halves(row_dot, query_pos, 1)
        for key_pos in range(2):
            key_part = halves(key_rows, key_pos, 0)
            value_part = halves(value_rows, key_pos, 0)
            key_seg = halves(segment, key_pos, 0)

            def accumulate(
                carry,
                query_part=query_part,
                query_seg=query_seg,
                grad_part=grad_part,
                norm_part=norm_part,
                dot_part=dot_part,
                key_part=key_part,
                value_part=value_part,
                key_seg=key_seg,
            ):
                part_query, part_key, part_value = carry
                scores = masked_scores(query_part, key_part, query_seg, key_seg)
                probs = jnp.exp(scores - norm_part[:, :, None])
                part_value = part_value + jnp.einsum(
                    "hqk,qhd->khd",
                    probs.astype(jnp.bfloat16),
                    grad_part,
                    preferred_element_type=jnp.float32,
                )
                grad_probs = jnp.einsum(
                    "qhd,khd->hqk", grad_part, value_part, preferred_element_type=jnp.float32
                )
                grad_scores = (probs * (grad_probs - dot_part[:, :, None])).astype(jnp.bfloat16)
                part_query = (
                    part_query
                    + jnp.einsum(
                        "hqk,khd->qhd", grad_scores, key_part, preferred_element_type=jnp.float32
                    )
                    * scale
                )
                part_key = (
                    part_key
                    + jnp.einsum(
                        "hqk,qhd->khd", grad_scores, query_part, preferred_element_type=jnp.float32
                    )
                    * scale
                )
                return (part_query, part_key, part_value)

            updated = lax.cond(
                touching(query_seg, key_seg),
                accumulate,
                keep_same,
                (query_grads[query_pos], key_grads[key_pos], value_grads[key_pos]),
            )
            query_grads[query_pos] = updated[0]
            key_grads[key_pos] = updated[1]
            value_grads[key_pos] = updated[2]
    return (
        jnp.concatenate(query_grads, axis=0),
        jnp.concatenate(key_grads, axis=0),
        jnp.concatenate(value_grads, axis=0),
    )


def local(
    frames,
    cotangent,
    segment_ids,
    norm_gain,
    norm_bias,
    w_qkv,
    qv_bias,
    w_out,
    out_bias,
    w_up,
    up_bias,
    w_down,
):
    rows, width = frames.shape
    seq_count, length = segment_ids.shape
    heads = H
    head_dim = width // heads
    shape_four = (seq_count, length, heads, head_dim)
    gathered = (
        lax.all_gather(norm_gain, "shard", axis=1, tiled=True),
        lax.all_gather(norm_bias, "shard", axis=1, tiled=True),
        lax.all_gather(w_qkv, "shard", axis=0, tiled=True),
        lax.all_gather(qv_bias, "shard", axis=1, tiled=True),
        lax.all_gather(w_out, "shard", axis=0, tiled=True),
        lax.all_gather(out_bias, "shard", axis=1, tiled=True),
    )
    gain_full = gathered[0].astype(jnp.float32)
    shift_full = gathered[1].astype(jnp.float32)
    qkv_full = gathered[2]
    qv_full = gathered[3].astype(jnp.float32)
    out_weight = gathered[4]
    outb_full = gathered[5].astype(jnp.float32)
    inputs = frames.astype(jnp.float32)
    unit_one, inverse_one = standardize(inputs)
    normed_one = (unit_one * gain_full[0] + shift_full[0]).astype(jnp.bfloat16)
    projected = jnp.dot(normed_one, qkv_full, preferred_element_type=jnp.float32)
    queries = (projected[:, :width] + qv_full[0]).astype(jnp.bfloat16).reshape(shape_four)
    key_rows = projected[:, width : 2 * width].astype(jnp.bfloat16).reshape(shape_four)
    value_rows = (projected[:, 2 * width :] + qv_full[1]).astype(jnp.bfloat16).reshape(shape_four)
    attended, log_norm = lax.map(attend_forward, (queries, key_rows, value_rows, segment_ids))
    mixed_low = attended.reshape(rows, width).astype(jnp.bfloat16)
    middle = (
        inputs + jnp.dot(mixed_low, out_weight, preferred_element_type=jnp.float32) + outb_full[0]
    )
    unit_two, inverse_two = standardize(middle)
    normed_two = (unit_two * gain_full[1] + shift_full[1]).astype(jnp.bfloat16)
    up_full, upb_full, down_full = (
        lax.all_gather(w_up, "shard", axis=1, tiled=True),
        lax.all_gather(up_bias, "shard", axis=0, tiled=True),
        lax.all_gather(w_down, "shard", axis=0, tiled=True),
    )
    hidden_pre = jnp.dot(normed_two, up_full, preferred_element_type=jnp.float32) + upb_full.astype(
        jnp.float32
    )
    activated = gelu_exact(hidden_pre).astype(jnp.bfloat16)
    branch_two = jnp.dot(activated, down_full, preferred_element_type=jnp.float32)
    result = middle + branch_two + outb_full[1]
    grad_out = cotangent.astype(jnp.float32)
    outb_grad_two = jnp.sum(grad_out, axis=0)
    up_back, down_back = (
        lax.all_gather(w_up, "shard", axis=1, tiled=True),
        lax.all_gather(w_down, "shard", axis=0, tiled=True),
    )
    grad_act = jnp.dot(cotangent, down_back.T, preferred_element_type=jnp.float32)
    grad_hidden = gelu_back(hidden_pre, grad_act).astype(jnp.bfloat16)
    down_grad = jnp.dot(activated.T, cotangent, preferred_element_type=jnp.float32)
    up_grad = jnp.dot(normed_two.T, grad_hidden, preferred_element_type=jnp.float32)
    upb_grad = jnp.sum(grad_hidden, axis=0, dtype=jnp.float32)
    grad_norm_two = jnp.dot(grad_hidden, up_back.T, preferred_element_type=jnp.float32)
    up_local, upb_local, down_local = (
        lax.psum_scatter(
            up_grad.astype(jnp.bfloat16), "shard", scatter_dimension=1, tiled=True
        ).astype(jnp.float32),
        lax.psum_scatter(
            upb_grad.astype(jnp.bfloat16), "shard", scatter_dimension=0, tiled=True
        ).astype(jnp.float32),
        lax.psum_scatter(
            down_grad.astype(jnp.bfloat16), "shard", scatter_dimension=0, tiled=True
        ).astype(jnp.float32),
    )
    up_summed, upb_summed, down_summed = (
        lax.psum(up_local.astype(jnp.bfloat16), "replica").astype(jnp.float32),
        lax.psum(upb_local.astype(jnp.bfloat16), "replica").astype(jnp.float32),
        lax.psum(down_local.astype(jnp.bfloat16), "replica").astype(jnp.float32),
    )
    gain_grad_two = jnp.sum(grad_norm_two * unit_two, axis=0)
    shift_grad_two = jnp.sum(grad_norm_two, axis=0)
    grad_middle = grad_out + norm_back(grad_norm_two * gain_full[1], unit_two, inverse_two)
    grad_branch = grad_middle.astype(jnp.bfloat16)
    outb_grad_one = jnp.sum(grad_branch, axis=0, dtype=jnp.float32)
    qkv_back, out_back = (
        lax.all_gather(w_qkv, "shard", axis=0, tiled=True),
        lax.all_gather(w_out, "shard", axis=0, tiled=True),
    )
    out_grad = jnp.dot(mixed_low.T, grad_branch, preferred_element_type=jnp.float32)
    grad_mixed = jnp.dot(grad_branch, out_back.T, preferred_element_type=jnp.float32).astype(
        jnp.bfloat16
    )
    grad_queries, grad_keys, grad_values = lax.map(
        attend_backward,
        (
            queries,
            key_rows,
            value_rows,
            segment_ids,
            log_norm,
            grad_mixed.reshape(shape_four),
            attended,
        ),
    )
    query_low = grad_queries.reshape(rows, width).astype(jnp.bfloat16)
    key_low = grad_keys.reshape(rows, width).astype(jnp.bfloat16)
    value_low = grad_values.reshape(rows, width).astype(jnp.bfloat16)
    grad_projected = jnp.concatenate([query_low, key_low, value_low], axis=1)
    qv_grad = jnp.stack(
        [
            jnp.sum(query_low, axis=0, dtype=jnp.float32),
            jnp.sum(value_low, axis=0, dtype=jnp.float32),
        ]
    )
    qkv_grad = jnp.dot(normed_one.T, grad_projected, preferred_element_type=jnp.float32)
    grad_norm_one = jnp.dot(grad_projected, qkv_back.T, preferred_element_type=jnp.float32)
    gain_grad_one = jnp.sum(grad_norm_one * unit_one, axis=0)
    shift_grad_one = jnp.sum(grad_norm_one, axis=0)
    grad_inputs = grad_middle + norm_back(grad_norm_one * gain_full[0], unit_one, inverse_one)
    gain_grads = jnp.stack([gain_grad_one, gain_grad_two])
    shift_grads = jnp.stack([shift_grad_one, shift_grad_two])
    outb_grads = jnp.stack([outb_grad_one, outb_grad_two])
    local_grads = (
        lax.psum_scatter(
            gain_grads.astype(jnp.bfloat16), "shard", scatter_dimension=1, tiled=True
        ).astype(jnp.float32),
        lax.psum_scatter(
            shift_grads.astype(jnp.bfloat16), "shard", scatter_dimension=1, tiled=True
        ).astype(jnp.float32),
        lax.psum_scatter(
            qkv_grad.astype(jnp.bfloat16), "shard", scatter_dimension=0, tiled=True
        ).astype(jnp.float32),
        lax.psum_scatter(
            qv_grad.astype(jnp.bfloat16), "shard", scatter_dimension=1, tiled=True
        ).astype(jnp.float32),
        lax.psum_scatter(
            out_grad.astype(jnp.bfloat16), "shard", scatter_dimension=0, tiled=True
        ).astype(jnp.float32),
        lax.psum_scatter(
            outb_grads.astype(jnp.bfloat16), "shard", scatter_dimension=1, tiled=True
        ).astype(jnp.float32),
    )
    summed = (
        lax.psum(local_grads[0].astype(jnp.bfloat16), "replica").astype(jnp.float32),
        lax.psum(local_grads[1].astype(jnp.bfloat16), "replica").astype(jnp.float32),
        lax.psum(local_grads[2].astype(jnp.bfloat16), "replica").astype(jnp.float32),
        lax.psum(local_grads[3].astype(jnp.bfloat16), "replica").astype(jnp.float32),
        lax.psum(local_grads[4].astype(jnp.bfloat16), "replica").astype(jnp.float32),
        lax.psum(local_grads[5].astype(jnp.bfloat16), "replica").astype(jnp.float32),
    )
    return (
        result.astype(jnp.bfloat16),
        grad_inputs,
        summed[0],
        summed[1],
        summed[2],
        summed[3],
        summed[4],
        summed[5],
        up_summed,
        upb_summed,
        down_summed,
    )


def solution(mesh):
    placed = (
        P(("replica", "shard"), None),
        P(("replica", "shard"), None),
        P(("replica", "shard"), None),
        P(None, "shard"),
        P(None, "shard"),
        P("shard", None),
        P(None, "shard"),
        P("shard", None),
        P(None, "shard"),
        P(None, "shard"),
        P("shard"),
        P("shard", None),
    )
    return jax.shard_map(
        local,
        mesh=mesh,
        in_specs=placed,
        out_specs=(
            P(("replica", "shard"), None),
            P(("replica", "shard"), None),
            P(None, "shard"),
            P(None, "shard"),
            P("shard", None),
            P(None, "shard"),
            P("shard", None),
            P(None, "shard"),
            P(None, "shard"),
            P("shard"),
            P("shard", None),
        ),
        check_vma=False,
    )
```

profile of v0, /device:TPU:0, one launch (start us, length us, event | category | flops | bytes accessed | tf_op | source)
XLA Modules:
  0.0 748.9 jit_solution(15768583942616573431)
XLA Ops:
  23.7 5.3 all_gather.31
  29.0 4.3 all_gather.32
  33.5 4.3 all_gather.34
  42.8 4.5 all-gather
  48.9 13.0 %all-gather.6.cloned.1.call-done = bf16[768,2304]{1,0:T(8,128)(2,1)} async-done(((bf16[384,2304]{1,0:T(8,128)(2,1)}), bf16[768,2304]{1,0:T(8,128)(2,1)}) %all-gather.6.cloned.1.call-update) | async-done | bytes 3538960 | tf_op jit(solution)/shard_map/all_gather | solution.py:211
  61.9 7.9 %fusion.108 = (bf16[1024,2304]{1,0:T(8,128)(2,1)}, f32[1024,2304]{1,0:T(8,128)S(1)}) fusion(bf16[768,2304]{1,0:T(8,128)(2,1)} %all-gather.6.cloned.1.call-done, bf16[1024,768]{0,1:T(8,128)(2,1)S(1)} %copy.79, f32[768]{0:T(1024)S(1)} %get-tuple-element.583, f32[768]{0:T(1024)S(1)} %get-tuple-element.581, f32[1024]{0:T(1024)S(1)} %add_rsqrt_fusion.1, ...), kind=kOutput, calls=%fused_computation.198 | convolution fusion | flops 3630956544 | bytes 19281920 | tf_op jit(solution)/shard_map/dot_general | solution.py:225
  82.3 7.4 conditional.12
  89.7 7.3 conditional.13
  97.8 8.4 %conditional.14 = (f32[512,12,64]{0,2,1:T(8,128)}) conditional(s32[]{:T(128)} %bitcast.14, () %tuple.120, (s32[512]{0:T(512)S(1)}, bf16[512,12,64]{0,2,1:T(8,128)(2,1)S(1)}, bf16[512,12,64]{0,2,1:T(8,128)(2,1)}, f32[12,512]{1,0:T(8,128)S(1)}, bf16[512,12,64]{0,2,1:T(8,128)(2,1)}) %tuple.314), branch_computations={%region_10.11_spmd, %region_11.12_spmd} | conditional | flops 818151424 | bytes 4483080 | solution.py:109
  98.1 8.1 %fusion.6 = f32[512,12,64]{0,2,1:T(8,128)} fusion(bf16[512,12,64]{0,2,1:T(8,128)(2,1)} %get-tuple-element.287, f32[12,512]{1,0:T(8,128)S(1)} %get-tuple-element.286, pred[512,512]{1,0:T(8,128)(4,1)S(1)} %broadcast_compare_fusion.2, bf16[512,12,64]{0,2,1:T(8,128)(2,1)S(1)} %get-tuple-element.284, bf16[512,12,64]{0,2,1:T(8,128)(2,1)} %get-tuple-element.285), kind=kOutput, calls=%fused_computation.15 | convolution fusion | flops 817889280 | bytes 4218880 | tf_op jit(solution)/shard_map/while/body/eval_jaxpr/cond/branch_1_fun/hqk,khd->qhd/dot_general | solution.py:105
  106.2 8.9 %conditional.15 = (f32[512,12,64]{0,2,1:T(8,128)}) conditional(s32[]{:T(128)} %bitcast.13, f32[512,12,64]{0,2,1:T(8,128)} %get-tuple-element.687, (s32[512]{0:T(512)S(1)}, s32[512]{0:T(512)S(1)}, bf16[512,12,64]{0,2,1:T(8,128)(2,1)S(1)}, bf16[512,12,64]{0,2,1:T(8,128)(2,1)S(1)}, f32[12,512]{1,0:T(8,128)S(1)}, ...), branch_computations={%region_12.13_spmd, %region_13.14_spmd} | conditional | flops 818544640 | bytes 6057992 | solution.py:109
  106.8 8.3 %bitcast_add_fusion = f32[512,12,64]{0,2,1:T(8,128)} fusion(f32[512,12,64]{0,2,1:T(8,128)} %get-tuple-element.288, bf16[512,12,64]{0,2,1:T(8,128)(2,1)} %get-tuple-element.294, f32[12,512]{1,0:T(8,128)S(1)} %get-tuple-element.293, pred[512,512]{1,0:T(8,128)(4,1)S(1)} %broadcast_compare_fusion.3, bf16[512,12,64]{0,2,1:T(8,128)(2,1)S(1)} %get-tuple-element.291, ...), kind=kOutput, calls=%fused_computation.23 | convolution fusion | flops 818282496 | bytes 5791744 | tf_op jit(solution)/shard_map/while/body/eval_jaxpr/cond/branch_1_fun/hqk,khd->qhd/dot_general | solution.py:105
  117.4 7.6 %conditional.16 = (f32[12,512]{1,0:T(8,128)}, f32[12,512]{1,0:T(8,128)S(1)}) conditional(s32[]{:T(128)} %bitcast.23, () %tuple.127, (s32[512]{0:T(512)S(1)}, s32[512]{0:T(512)S(1)}, bf16[512,12,64]{0,2,1:T(8,128)(2,1)}, bf16[512,12,64]{0,2,1:T(8,128)(2,1)}) %tuple.316), branch_computations={%region_14.15_spmd, %region_15.0_spmd} | conditional | flops 424953856 | bytes 27725840 | solution.py:86
  125.1 8.4 %conditional.17 = ((f32[12,512]{1,0:T(8,128)}, f32[12,512]{1,0:T(8,128)S(1)})) conditional(s32[]{:T(128)} %bitcast.22, (f32[12,512]{1,0:T(8,128)}, f32[12,512]{1,0:T(8,128)S(1)}) %conditional.16, (s32[512]{0:T(512)S(1)}, bf16[512,12,64]{0,2,1:T(8,128)(2,1)}, bf16[512,12,64]{0,2,1:T(8,128)(2,1)S(1)}, f32[12,512]{1,0:T(8,128)}, ...), branch_computations={%region_18.19_spmd, %region_19.0_spmd} | conditional | flops 424947712 | bytes 27846680 | solution.py:86
  134.2 8.3 %conditional.18 = (f32[512,12,64]{0,2,1:T(8,128)}) conditional(s32[]{:T(128)} %bitcast.23, () %tuple.126, (s32[512]{0:T(512)S(1)}, s32[512]{0:T(512)S(1)}, bf16[512,12,64]{0,2,1:T(8,128)(2,1)}, bf16[512,12,64]{0,2,1:T(8,128)(2,1)S(1)}, f32[12,512]{1,0:T(8,128)S(1)}, /*index=5*/bf16[512,12,64]{0,2,1:T(8,128)(2,1)}) %tuple.317), branch_computations={%region_22.23_spmd, %region_23.24_spmd} | conditional | flops 818151424 | bytes 4485128 | solution.py:109
  134.5 8.0 %fusion.21 = f32[512,12,64]{0,2,1:T(8,128)} fusion(bf16[512,12,64]{0,2,1:T(8,128)(2,1)} %get-tuple-element.309, f32[12,512]{1,0:T(8,128)S(1)} %get-tuple-element.308, pred[512,512]{1,0:T(8,128)(4,1)S(1)} %broadcast_compare_fusion.6, bf16[512,12,64]{0,2,1:T(8,128)(2,1)} %get-tuple-element.306, bf16[512,12,64]{0,2,1:T(8,128)(2,1)S(1)} %get-tuple-element.307), kind=kOutput, calls=%fused_computation.42 | convolution fusion | flops 817889280 | bytes 4218880 | tf_op jit(solution)/shard_map/while/body/eval_jaxpr/cond/branch_1_fun/hqk,khd->qhd/dot_general | solution.py:105
  142.5 9.0 %conditional.19 = (f32[512,12,64]{0,2,1:T(8,128)}) conditional(s32[]{:T(128)} %bitcast.22, f32[512,12,64]{0,2,1:T(8,128)} %get-tuple-element.690, (s32[512]{0:T(512)S(1)}, bf16[512,12,64]{0,2,1:T(8,128)(2,1)}, bf16[512,12,64]{0,2,1:T(8,128)(2,1)S(1)}, f32[12,512]{1,0:T(8,128)S(1)}, bf16[512,12,64]{0,2,1:T(8,128)(2,1)}, ...), branch_computations={%region_24.25_spmd, %region_25.26_spmd} | conditional | flops 818544640 | bytes 6055944 | solution.py:109
  142.9 8.6 %bitcast_add_fusion.1 = f32[512,12,64]{0,2,1:T(8,128)} fusion(f32[512,12,64]{0,2,1:T(8,128)} %get-tuple-element.310, bf16[512,12,64]{0,2,1:T(8,128)(2,1)} %get-tuple-element.315, f32[12,512]{1,0:T(8,128)S(1)} %get-tuple-element.314, pred[512,512]{1,0:T(8,128)(4,1)S(1)} %broadcast_compare_fusion.7, bf16[512,12,64]{0,2,1:T(8,128)(2,1)} %get-tuple-element.312, ...), kind=kOutput, calls=%fused_computation.50 | convolution fusion | flops 818282496 | bytes 5791744 | tf_op jit(solution)/shard_map/while/body/eval_jaxpr/cond/branch_1_fun/hqk,khd->qhd/dot_general | solution.py:105
  159.3 39.0 %multiply_convert_fusion.4 = (bf16[1024,3072]{1,0:T(8,128)(2,1)}, f32[1024,3072]{1,0:T(8,128)}, f32[1024,3072]{1,0:T(8,128)}) fusion(f32[3072]{0:T(1024)S(1)} %bitcast.201, bf16[768,3072]{1,0:T(8,128)(2,1)} %all-gather.10.cloned.1.call-done, f32[1024,768]{0,1:T(8,128)} %copy-done.8, f32[768]{0:T(1024)S(1)} %get-tuple-element.582, ...), kind=kOutput, calls=%fused_computation.101 | convolution fusion | flops 5043388416 | bytes 39348224 | tf_op jit(solution)/shard_map/dot_general | solution.py:241
  198.3 16.4 %all-gather.12.cloned.1.call-done = bf16[3072,768]{1,0:T(8,128)(2,1)} async-done(((bf16[1536,768]{1,0:T(8,128)(2,1)}), bf16[3072,768]{1,0:T(8,128)(2,1)}) %all-gather.12.cloned.1.call-update) | async-done | bytes 4718608 | tf_op jit(solution)/shard_map/all_gather | solution.py:239
  214.6 17.3 %fusion.112 = (bf16[3072]{0:T(1024)(128)(2,1)}, bf16[1024,3072]{1,0:T(8,128)(2,1)}) fusion(f32[1024,3072]{1,0:T(8,128)} %get-tuple-element.602, bf16[1024,768]{1,0:T(8,128)(2,1)S(1)} %copy-done.23, bf16[3072,768]{1,0:T(8,128)(2,1)} %all-gather.12.cloned.1.call-done, f32[1024,3072]{1,0:T(8,128)} %get-tuple-element.633, f32[3072]{0:T(1024)S(1)} %bitcast.202), kind=kOutput, calls=%fused_computation.202 | convolution fusion | flops 4882166784 | bytes 37767168 | tf_op jit(solution)/shard_map/dot_general | solution.py:253
  232.0 10.5 %fusion.110 = (bf16[768]{0:T(1024)(128)(2,1)}, f32[1024,768]{1,0:T(8,128)}) fusion(bf16[1024,3072]{1,0:T(8,128)(2,1)} %get-tuple-element.639, bf16[768,3072]{1,0:T(8,128)(2,1)} %all-gather.10.cloned.1.call-done), kind=kOutput, calls=%fused_computation.200 | convolution fusion | flops 4832623616 | bytes 14157312 | tf_op jit(solution)/shard_map/dot_general | solution.py:258
  260.8 14.6 %conditional.20 = (f32[512,12,64]{0,2,1:T(8,128)}, f32[512,12,64]{0,2,1:T(8,128)S(1)}, f32[512,12,64]{0,2,1:T(8,128)S(1)}) conditional(s32[]{:T(128)} %bitcast.14, () %tuple.132, (s32[512]{0:T(512)S(1)}, bf16[512,12,64]{0,2,1:T(8,128)(2,1)S(1)}, bf16[512,12,64]{0,2,1:T(8,128)(2,1)S(1)}, f32[12,512]{1,0:T(8,128)S(1)}, ...), branch_computations={%region_31.32_spmd.clone, %region_32.33_spmd.clone} | conditional | flops 2045771776 | bytes 77146216 | solution.py:173
  262.9 4.8 multiply_convert_fusion.3
  277.1 16.9 %conditional.21 = (f32[512,12,64]{0,2,1:T(8,128)}, f32[512,12,64]{0,2,1:T(8,128)S(1)}, f32[512,12,64]{0,2,1:T(8,128)}) conditional(s32[]{:T(128)} %bitcast.13, f32[512,12,64]{0,2,1:T(8,128)} %get-tuple-element.394, (s32[512]{0:T(512)S(1)}, s32[512]{0:T(512)S(1)}, bf16[512,12,64]{0,2,1:T(8,128)(2,1)S(1)}, bf16[512,12,64]{0,2,1:T(8,128)(2,1)S(1)}, ...), branch_computations={%region_33.34_spmd, %region_34.35_spmd} | conditional | flops 2046164992 | bytes 75575376 | solution.py:173
  279.1 4.8 multiply_convert_fusion
  284.0 4.6 bitcast_add_fusion.2
  295.2 18.5 %conditional.22 = (f32[512,12,64]{0,2,1:T(8,128)}, f32[512,12,64]{0,2,1:T(8,128)}, f32[512,12,64]{0,2,1:T(8,128)}) conditional(s32[]{:T(128)} %bitcast.23, (f32[512,12,64]{0,2,1:T(8,128)}, f32[512,12,64]{0,2,1:T(8,128)}) %tuple.289, (s32[512]{0:T(512)S(1)}, s32[512]{0:T(512)S(1)}, bf16[512,12,64]{0,2,1:T(8,128)(2,1)}, ...), branch_computations={%region_35.36_spmd, %region_36.37_spmd} | conditional | flops 2046558208 | bytes 105459936 | solution.py:173
  298.9 4.8 multiply_convert_fusion.1
  313.7 21.3 %conditional.23 = (f32[512,12,64]{0,2,1:T(8,128)}, f32[512,12,64]{0,2,1:T(8,128)}, f32[512,12,64]{0,2,1:T(8,128)}) conditional(s32[]{:T(128)} %bitcast.22, (f32[512,12,64]{0,2,1:T(8,128)}, f32[512,12,64]{0,2,1:T(8,128)}, f32[512,12,64]{0,2,1:T(8,128)}) %tuple.287, (s32[512]{0:T(512)S(1)}, bf16[512,12,64]{0,2,1:T(8,128)(2,1)}, ...), branch_computations={%region_37.38_spmd, %region_38.39_spmd} | conditional | flops 2046951424 | bytes 91302032 | solution.py:173
  317.2 4.8 multiply_convert_fusion.2
  324.3 5.1 bitcast_add_fusion.7
  329.5 5.5 bitcast_add_fusion.6
  343.2 5.9 convolution_convert_fusion.2
  349.2 9.7 %convolution_convert_fusion.1 = bf16[768,3072]{1,0:T(8,128)(2,1)} fusion(bf16[1024,3072]{1,0:T(8,128)(2,1)} %get-tuple-element.639, f32[1024,768]{0,1:T(8,128)} %copy-done.8, f32[768]{0:T(1024)S(1)} %copy-done.68, f32[768]{0:T(1024)S(1)} %get-tuple-element.580, f32[1024]{0:T(1024)S(1)} %add_rsqrt_fusion, f32[1024]{0:T(1024)S(1)} %broadcast_multiply_fusion.4), kind=kOutput, calls=%fused_computation.116 | convolution fusion | flops 4838129664 | bytes 14170112 | tf_op jit(solution)/shard_map/dot_general | solution.py:256
  360.3 9.6 %convolution_convert_fusion = bf16[3072,768]{1,0:T(8,128)(2,1)} fusion(bf16[1024,3072]{1,0:T(8,128)(2,1)} %get-tuple-element.601, bf16[1024,768]{1,0:T(8,128)(2,1)S(1)} %copy-done.24), kind=kOutput, calls=%fused_computation.115 | convolution fusion | flops 4834197504 | bytes 12582912 | tf_op jit(solution)/shard_map/dot_general | solution.py:255
  371.4 9.0 %fusion.111 = (bf16[768]{0:T(1024)(128)(2,1)S(1)}, f32[1024,768]{1,0:T(8,128)}) fusion(bf16[768,2304]{1,0:T(8,128)(2,1)} %all-gather.6.cloned.1.call-done, bf16[1024,768]{0,1:T(8,128)(2,1)} %bitcast.159, bf16[1024,768]{0,1:T(8,128)(2,1)} %bitcast.155, bf16[1024,768]{0,1:T(8,128)(2,1)} %bitcast.157), kind=kOutput, calls=%fused_computation.201 | convolution fusion | flops 3638820096 | bytes 11404800 | tf_op jit(solution)/shard_map/dot_general | solution.py:311
  390.1 6.9 reduce-scatter.17.cloned.1.call-done
  397.0 62.9 %reduce-scatter.21.cloned.1.call-done = bf16[768,1536]{1,0:T(8,128)(2,1)} async-done(((bf16[768,3072]{1,0:T(8,128)(2,1)}), bf16[768,1536]{1,0:T(8,128)(2,1)}) %reduce-scatter.21.cloned.1.call-update) | async-done | bytes 2359312 | tf_op jit(solution)/shard_map/reduce_scatter | solution.py:260
  459.8 63.0 %reduce-scatter.23.cloned.1.call-done = bf16[1536,768]{1,0:T(8,128)(2,1)} async-done(((bf16[3072,768]{1,0:T(8,128)(2,1)}), bf16[1536,768]{1,0:T(8,128)(2,1)}) %reduce-scatter.23.cloned.1.call-update) | async-done | bytes 2359312 | tf_op jit(solution)/shard_map/reduce_scatter | solution.py:266
  524.2 5.5 fusion.81
  533.4 9.5 %add_convert_fusion.1 = bf16[1024,768]{0,1:T(8,128)(2,1)} fusion(f32[1024,768]{0,1:T(8,128)S(1)} %copy-done.10, bf16[1024,3072]{1,0:T(8,128)(2,1)} %get-tuple-element.601, bf16[3072,768]{1,0:T(8,128)(2,1)} %all-gather.12.cloned.1.call-done, f32[768]{0:T(1024)S(1)} %copy-done.66), kind=kOutput, calls=%fused_computation.149 | convolution fusion | flops 4834197504 | bytes 15731712 | tf_op jit(solution)/shard_map/dot_general | solution.py:245
  545.5 5.0 all-reduce
  552.5 9.8 %reduce-scatter.25.cloned.1.call-done = bf16[384,2]{1,0:T(8,128)(2,1)} async-done(((bf16[768,2]{1,0:T(8,128)(2,1)}), bf16[384,2]{1,0:T(8,128)(2,1)}) %reduce-scatter.25.cloned.1.call-update) | async-done | bytes 1552
  563.3 12.1 %reduce-scatter.31.cloned.1.call-done = bf16[384,2]{1,0:T(8,128)(2,1)} async-done(((bf16[768,2]{1,0:T(8,128)(2,1)}), bf16[384,2]{1,0:T(8,128)(2,1)}) %reduce-scatter.31.cloned.1.call-update) | async-done | bytes 1552
  576.4 64.0 %all-reduce.1 = (bf16[2,384]{1,0:T(2,128)(2,1)S(1)}, bf16[2,384]{1,0:T(2,128)(2,1)S(1)}, bf16[2,384]{1,0:T(2,128)(2,1)S(1)}, bf16[2,384]{1,0:T(2,128)(2,1)S(1)}, bf16[1536]{0:T(1024)(128)(2,1)S(1)}) all-reduce(bf16[2,384]{1,0:T(2,128)(2,1)S(1)} %copy.96, ...), channel_id=1, replica_groups=mesh['replica'=16,'shard'=2] {'replica'}, use_global_device_ids=true, to_apply=%region_44.45 | all-reduce | flops 4608 | bytes 18432 | tf_op jit(solution)/shard_map/psum | solution.py:339
  643.4 88.3 %all-reduce.5.cloned.1.call-done = (bf16[384,2304]{1,0:T(8,128)(2,1)}, bf16[384,768]{1,0:T(8,128)(2,1)}, bf16[768,1536]{1,0:T(8,128)(2,1)}, bf16[1536,768]{1,0:T(8,128)(2,1)}) async-done(((bf16[384,2304]{1,0:T(8,128)(2,1)}, bf16[384,768]{1,0:T(8,128)(2,1)}, bf16[768,1536]{1,0:T(8,128)(2,1)}, bf16[1536,768]{1,0:T(8,128)(2,1)}), (bf16[384,2304]{1,0:T(8,128)(2,1)}, bf16[384,768]{1,0:T(8,128)(2,1)}, ...) | async-done | bytes 7077904 | tf_op jit(solution)/shard_map/psum | solution.py:341
  731.6 4.6 convert_element_type.275
  (319 shorter events, 164.5 us)
Async XLA Ops:
  7.2 54.7 %all-gather.6.cloned.1.call-start = ((), (), s32[]{:S(2)}) async-start(), calls=%async_computation.8 | async-start | bytes 5308416 | tf_op jit(solution)/shard_map/all_gather | solution.py:211
  7.9 145.7 %all-gather.8.cloned.1.call-start = ((), (), s32[]{:S(2)}) async-start(), calls=%async_computation.9 | async-start | bytes 1769472 | tf_op jit(solution)/shard_map/all_gather | solution.py:213
  8.7 150.6 %all-gather.10.cloned.1.call-start = ((), (), s32[]{:S(2)}) async-start(), calls=%async_computation.10 | async-start | bytes 7077888 | tf_op jit(solution)/shard_map/all_gather | solution.py:237
  9.4 14.3 %copy-start.73 = (bf16[2,384]{1,0:T(2,128)(2,1)S(1)}, bf16[2,384]{1,0:T(2,128)(2,1)}, u32[]{:S(2)}) copy-start(bf16[2,384]{1,0:T(2,128)(2,1)} %param.39) | copy-start | bytes 4612
  9.4 19.6 %copy-start.74 = (bf16[2,384]{1,0:T(2,128)(2,1)S(1)}, bf16[2,384]{1,0:T(2,128)(2,1)}, u32[]{:S(2)}) copy-start(bf16[2,384]{1,0:T(2,128)(2,1)} %param.40) | copy-start | bytes 4612
  9.4 24.0 %copy-start.75 = (bf16[2,384]{1,0:T(2,128)(2,1)S(1)}, bf16[2,384]{1,0:T(2,128)(2,1)}, u32[]{:S(2)}) copy-start(bf16[2,384]{1,0:T(2,128)(2,1)} %param.42) | copy-start | bytes 4612
  9.4 28.4 %copy-start.76 = (bf16[2,384]{1,0:T(2,128)(2,1)S(1)}, bf16[2,384]{1,0:T(2,128)(2,1)}, u32[]{:S(2)}) copy-start(bf16[2,384]{1,0:T(2,128)(2,1)} %param.44) | copy-start | bytes 4612
  9.4 33.4 %copy-start.71 = (bf16[1536]{0:T(1024)(128)(2,1)S(1)}, bf16[1536]{0:T(1024)(128)(2,1)}, u32[]{:S(2)}) copy-start(bf16[1536]{0:T(1024)(128)(2,1)} %param.46) | copy-start | bytes 9220
  9.5 37.9 %copy-start.22 = (bf16[1024,768]{1,0:T(8,128)(2,1)S(1)}, bf16[1024,768]{1,0:T(8,128)(2,1)}, u32[]{:S(2)}) copy-start(bf16[1024,768]{1,0:T(8,128)(2,1)} %param.37) | copy-start | bytes 4718596
  9.5 205.2 %all-gather.12.cloned.1.call-start = ((), (), s32[]{:S(2)}) async-start(), calls=%async_computation.11 | async-start | bytes 7077888 | tf_op jit(solution)/shard_map/all_gather | solution.py:239
  10.0 380.0 %reduce-scatter.19.cloned.1.call-start = ((), (), s32[]{:S(2)}) async-start(), calls=%async_computation.13 | async-start | bytes 1769472 | tf_op jit(solution)/shard_map/reduce_scatter | solution.py:331
  10.1 124.1 %copy-start.51 = (s32[1,512]{1,0:T(1,128)}, s32[1,512]{1,0:T(1,128)S(1)}, u32[]{:S(2)}) copy-start(s32[1,512]{1,0:T(1,128)S(1)} %get-tuple-element.623) | copy-start | bytes 6148
  10.1 132.4 %copy-start.49 = (s32[1,512]{1,0:T(1,128)}, s32[1,512]{1,0:T(1,128)S(1)}, u32[]{:S(2)}) copy-start(s32[1,512]{1,0:T(1,128)S(1)} %get-tuple-element.624) | copy-start | bytes 6148
  22.9 130.8 %copy-start.2 = (bf16[1024,768]{0,1:T(8,128)(2,1)}, bf16[1024,768]{0,1:T(8,128)(2,1)S(1)}, u32[]{:S(2)}) copy-start(bf16[1024,768]{0,1:T(8,128)(2,1)S(1)} %copy.79) | copy-start | bytes 4718596
  23.2 46.6 %copy-start.53 = (f32[1024]{0:T(1024)}, f32[1024]{0:T(1024)S(1)}, u32[]{:S(2)}) copy-start(f32[1024]{0:T(1024)S(1)} %broadcast_multiply_fusion.5) | copy-start | bytes 12292
  23.7 46.2 %copy-start.57 = (f32[1024]{0:T(1024)}, f32[1024]{0:T(1024)S(1)}, u32[]{:S(2)}) copy-start(f32[1024]{0:T(1024)S(1)} %add_rsqrt_fusion.1) | copy-start | bytes 12292
  29.0 40.8 %copy-start.55 = (f32[768]{0:T(1024)}, f32[768]{0:T(1024)S(1)}, u32[]{:S(2)}) copy-start(f32[768]{0:T(1024)S(1)} %get-tuple-element.581) | copy-start | bytes 9220
  33.4 36.4 %copy-start.69 = (f32[768]{0:T(1024)}, f32[768]{0:T(1024)S(1)}, u32[]{:S(2)}) copy-start(f32[768]{0:T(1024)S(1)} %get-tuple-element.583) | copy-start | bytes 9220
  33.4 125.8 %copy-start.67 = (f32[768]{0:T(1024)}, f32[768]{0:T(1024)S(1)}, u32[]{:S(2)}) copy-start(f32[768]{0:T(1024)S(1)} %get-tuple-element.582) | copy-start | bytes 9220
  72.2 34.0 %copy-start = (bf16[512,768]{0,1:T(8,128)(2,1)}, bf16[512,768]{0,1:T(8,128)(2,1)S(1)}, u32[]{:S(2)}) copy-start(bf16[512,768]{0,1:T(8,128)(2,1)S(1)} %copy.80) | copy-start | bytes 2359300
  77.4 65.1 %copy-start.4 = (bf16[512,768]{0,1:T(8,128)(2,1)}, bf16[512,768]{0,1:T(8,128)(2,1)S(1)}, u32[]{:S(2)}) copy-start(bf16[512,768]{0,1:T(8,128)(2,1)S(1)} %copy.82) | copy-start | bytes 2359300
  97.8 8.4 %copy-start.59 = (f32[12,512]{1,0:T(8,128)}, f32[12,512]{1,0:T(8,128)S(1)}, u32[]{:S(2)}) copy-start(f32[12,512]{1,0:T(8,128)S(1)} %log_add_fusion.1) | copy-start | bytes 73732
  125.0 9.1 %copy-start.6 = (bf16[512,768]{0,1:T(8,128)(2,1)S(1)}, bf16[512,768]{0,1:T(8,128)(2,1)}, u32[]{:S(2)}) copy-start(bf16[512,768]{0,1:T(8,128)(2,1)} %copy.81) | copy-start | bytes 2359300
  134.2 8.3 %copy-start.61 = (f32[12,512]{1,0:T(8,128)}, f32[12,512]{1,0:T(8,128)S(1)}, u32[]{:S(2)}) copy-start(f32[12,512]{1,0:T(8,128)S(1)} %log_add_fusion) | copy-start | bytes 73732
  159.3 55.3 %copy-start.23 = (bf16[1024,768]{1,0:T(8,128)(2,1)S(1)}, bf16[1024,768]{1,0:T(8,128)(2,1)}, u32[]{:S(2)}) copy-start(bf16[1024,768]{1,0:T(8,128)(2,1)} %param.37) | copy-start | bytes 4718596
  255.3 141.6 %reduce-scatter.17.cloned.1.call-start = ((), (), s32[]{:S(2)}) async-start(), calls=%async_computation.12 | async-start | bytes 5308416 | tf_op jit(solution)/shard_map/reduce_scatter | solution.py:325
  260.8 14.7 %copy-start.5 = (bf16[512,768]{0,1:T(8,128)(2,1)S(1)}, bf16[512,768]{0,1:T(8,128)(2,1)}, u32[]{:S(2)}) copy-start(bf16[512,768]{0,1:T(8,128)(2,1)} %copy-done.4) | copy-start | bytes 2359300
  260.8 14.7 %copy-start.37 = (bf16[512,768]{0,1:T(8,128)(2,1)S(1)}, bf16[512,768]{0,1:T(8,128)(2,1)}, u32[]{:S(2)}) copy-start(bf16[512,768]{0,1:T(8,128)(2,1)} %copy.84) | copy-start | bytes 2359300
  260.8 14.7 %copy-start.50 = (s32[1,512]{1,0:T(1,128)S(1)}, s32[1,512]{1,0:T(1,128)}, u32[]{:S(2)}) copy-start(s32[1,512]{1,0:T(1,128)} %copy-done.49) | copy-start | bytes 6148
  275.5 18.5 %copy-start.62 = (f32[12,512]{1,0:T(8,128)S(1)}, f32[12,512]{1,0:T(8,128)}, u32[]{:S(2)}) copy-start(f32[12,512]{1,0:T(8,128)} %copy-done.61) | copy-start | bytes 73732
  298.9 4.8 copy-start.13
  306.0 6.5 copy-start.14
  313.7 22.8 %copy-start.15 = (f32[512,12,64]{0,2,1:T(8,128)S(1)}, f32[512,12,64]{0,2,1:T(8,128)}, u32[]{:S(2)}) copy-start(f32[512,12,64]{0,2,1:T(8,128)} %get-tuple-element.403) | copy-start | bytes 4718596
  317.2 4.8 copy-start.17
  324.3 5.1 copy-start.18
  343.2 6.0 copy-start.68
  349.1 110.7 %reduce-scatter.21.cloned.1.call-start = ((), (), s32[]{:S(2)}) async-start(), calls=%async_computation.14 | async-start | bytes 7077888 | tf_op jit(solution)/shard_map/reduce_scatter | solution.py:260
  358.9 163.9 %reduce-scatter.23.cloned.1.call-start = ((), (), s32[]{:S(2)}) async-start(), calls=%async_computation.15 | async-start | bytes 7077888 | tf_op jit(solution)/shard_map/reduce_scatter | solution.py:266
  370.0 180.6 %reduce-scatter.29.cloned.1.call-start = ((), (), s32[]{:S(2)}) async-start(), calls=%async_computation.18 | async-start | bytes 294912
  371.4 9.0 %copy-start.72 = (bf16[768]{0:T(1024)(128)(2,1)S(1)}, bf16[768]{0:T(1024)(128)(2,1)}, u32[]{:S(2)}) copy-start(bf16[768]{0:T(1024)(128)(2,1)} %get-tuple-element.634) | copy-start | bytes 4612
  380.4 7.4 copy-start.64
  386.9 136.0 %copy-start.78 = (u32[32]{0:T(128)S(1)}, u32[32]{0:T(128)}, u32[]{:S(2)}) copy-start(u32[32]{0:T(128)} %constant.209) | copy-start | bytes 388
  386.9 164.6 %reduce-scatter.27.cloned.1.call-start = ((), (), s32[]{:S(2)}) async-start(), calls=%async_computation.17 | async-start | bytes 294912
  387.9 174.5 %reduce-scatter.25.cloned.1.call-start = ((), (), s32[]{:S(2)}) async-start(), calls=%async_computation.16 | async-start | bytes 294912
  388.8 186.6 %reduce-scatter.31.cloned.1.call-start = ((), (), s32[]{:S(2)}) async-start(), calls=%async_computation.19 | async-start | bytes 294912
  389.8 341.9 %all-reduce.5.cloned.1.call-start = ((), (), s32[]{:S(2)}) async-start(), calls=%async_computation.20 | async-start | bytes 14155776 | tf_op jit(solution)/shard_map/psum | solution.py:341
  533.4 12.1 %copy-start.65 = (bf16[3072]{0:T(1024)(128)(2,1)S(1)}, bf16[3072]{0:T(1024)(128)(2,1)}, u32[]{:S(2)}) copy-start(bf16[3072]{0:T(1024)(128)(2,1)} %get-tuple-element.638) | copy-start | bytes 18436
  731.6 4.7 copy-start.30
  (44 other events, 125.6 us)
Sparse Core Ops, SparseCore 0:
  9.6 52.3 all-gather.5
  63.5 22.7 all-gather.7
  87.8 62.6 all-gather.9
  151.9 62.6 all-gather.11
  255.4 21.7 reduce-scatter.18
  349.3 47.6 reduce-scatter.16
  399.8 59.9 reduce-scatter.20
  462.8 60.0 reduce-scatter.22
  525.1 10.9 reduce-scatter.28
  538.2 10.9 reduce-scatter.26
  551.4 10.9 reduce-scatter.24
  564.5 10.9 reduce-scatter.30
  579.5 152.0 all-reduce.4
where the time goes:
time: 759 us; the launch traced here: 749 us
  waiting for transfers between devices  275 us (36%)
  matrix products  241 us (32%)
  blocking collectives  91.8 us (12%)
  other arithmetic  58.7 us (8%)
  local copies, waits for them, and re-layouts  52.9 us (7%)
  between operations  26.3 us (3%)
    psum x1, waiting for transfers between devices, local(): lax.psum(local_grads[2].astype(jnp.bfloat16), 'replica').astype(jnp.float32)  88.3 us
    psum x1, blocking collectives, local(): lax.psum(local_grads[0].astype(jnp.bfloat16), 'replica').astype(jnp.float32)  64 us
    reduce_scatter x1, waiting for transfers between devices, local(): lax.psum_scatter(down_grad.astype(jnp.bfloat16), 'shard', scatter_dimensi...  63 us
    reduce_scatter x1, waiting for transfers between devices, local(): lax.psum_scatter(up_grad.astype(jnp.bfloat16), 'shard', scatter_dimension...  62.9 us
    dot_general x1, matrix products, local(): jnp.dot(normed_two, up_full, preferred_element_type=jnp.float32)  39 us
    dot_general x4, matrix products, spread(): jnp.einsum('hqk,khd->qhd', weights, value_part, preferred_element_type=jn...  33 us
    unnamed x141, local copies, waits for them, and re-layouts  26.3 us
    unnamed x17, waiting for transfers between devices  24.7 us
  transfers between devices with their start and end apart: 13, of which 8 were waited for; matrix products, arithmetic and copies ran while one was open for 39% of the time, Pallas kernels for 0%

commit v1 on v0

--- a/solution.py
+++ b/solution.py
@@ -7,6 +7,12 @@
 H = 12
 EPS = 1e-05
 NEG = -1e30
+
+
+def add_all(shard, name):
+    parts = lax.all_gather(shard, name, axis=0, tiled=False)
+    result = parts.sum(axis=0)
+    return result
 
 
 def standardize(values):
@@ -338,7 +344,7 @@
     summed = (
         lax.psum(local_grads[0].astype(jnp.bfloat16), "replica").astype(jnp.float32),
         lax.psum(local_grads[1].astype(jnp.bfloat16), "replica").astype(jnp.float32),
-        lax.psum(local_grads[2].astype(jnp.bfloat16), "replica").astype(jnp.float32),
+        add_all(local_grads[2].astype(jnp.bfloat16), "replica").astype(jnp.float32),
         lax.psum(local_grads[3].astype(jnp.bfloat16), "replica").astype(jnp.float32),
         lax.psum(local_grads[4].astype(jnp.bfloat16), "replica").astype(jnp.float32),
         lax.psum(local_grads[5].astype(jnp.bfloat16), "replica").astype(jnp.float32),

time: 759 us -> 811 us (1.069)
  waiting for transfers between devices: 275 us -> 326 us
  other arithmetic: 58.7 us -> 70.3 us
  matrix products: 241 us -> 230 us
    all_gather x0 -> x1, waiting for transfers between devices: none -> 135 us  [add_all(): parts = lax.all_gather(shard, name, axis=0, tiled=False)]
    reduce_scatter x1, waiting for transfers between devices: 62.9 us -> 0.02 us  [local(): lax.psum_scatter(up_grad.astype(jnp.bfloat16), 'shard', scatter_dimension...]
    reduce_scatter x1, waiting for transfers between devices: 63 us -> 18.4 us  [local(): lax.psum_scatter(down_grad.astype(jnp.bfloat16), 'shard', scatter_dimensi...]
    reduce_scatter x1, waiting for transfers between devices: 6.87 us -> 50.6 us  [local(): lax.psum_scatter(qkv_grad.astype(jnp.bfloat16), 'shard', scatter_dimensio...]
    psum x1, waiting for transfers between devices: 88.3 us -> 63.1 us  [local(): lax.psum(local_grads[4].astype(jnp.bfloat16), 'replica').astype(jnp.float32)]
    reduce_sum x0 -> x1, other arithmetic: none -> 10.2 us  [add_all(): result = parts.sum(axis=0)]
    unnamed x17 -> x18, waiting for transfers between devices: 24.7 us -> 26.4 us
    unnamed x141 -> x135, local copies, waits for them, and re-layouts: 26.3 us -> 27.2 us
  transfers between devices with their start and end apart: 13 -> 14, of which waited for: 8 -> 8; matrix products, arithmetic and copies ran while one was open for 39% -> 36% of each run, Pallas kernels for 0% -> 0%
where the time goes in v1:
time: 811 us; the launch traced here: 801 us
  waiting for transfers between devices  326 us (40%)
  matrix products  230 us (28%)
  blocking collectives  91 us (11%)
  other arithmetic  70.3 us (9%)
  local copies, waits for them, and re-layouts  54.9 us (7%)
  between operations  26.1 us (3%)
    all_gather x1, waiting for transfers between devices, add_all(): parts = lax.all_gather(shard, name, axis=0, tiled=False)  135 us
    psum x1, blocking collectives, local(): lax.psum(local_grads[0].astype(jnp.bfloat16), 'replica').astype(jnp.float32)  63.3 us
    psum x1, waiting for transfers between devices, local(): lax.psum(local_grads[4].astype(jnp.bfloat16), 'replica').astype(jnp.float32)  63.1 us
    reduce_scatter x1, waiting for transfers between devices, local(): lax.psum_scatter(qkv_grad.astype(jnp.bfloat16), 'shard', scatter_dimensio...  50.6 us
    dot_general x1, matrix products, local(): jnp.dot(normed_two, up_full, preferred_element_type=jnp.float32)  38.9 us
    dot_general x4, matrix products, spread(): jnp.einsum('hqk,khd->qhd', weights, value_part, preferred_element_type=jn...  32.8 us
    unnamed x135, local copies, waits for them, and re-layouts  27.2 us
    unnamed x18, waiting for transfers between devices  26.4 us
  transfers between devices with their start and end apart: 14, of which 8 were waited for; matrix products, arithmetic and copies ran while one was open for 36% of the time, Pallas kernels for 0%

profile of v1, /device:TPU:0, one launch (start us, length us, event | category | flops | bytes accessed | tf_op | source)
XLA Modules:
  0.0 800.8 jit_solution(3456188086604275943)
XLA Ops:
  21.1 5.3 all_gather.42
  28.7 4.3 all_gather.38
  33.1 4.3 all_gather.37
  42.7 4.5 all-gather.1
  48.8 13.1 %all-gather.8.cloned.1.call-done = bf16[768,2304]{1,0:T(8,128)(2,1)} async-done(((bf16[384,2304]{1,0:T(8,128)(2,1)}), bf16[768,2304]{1,0:T(8,128)(2,1)}) %all-gather.8.cloned.1.call-update) | async-done | bytes 3538960 | tf_op jit(solution)/shard_map/all_gather | solution.py:217
  62.0 7.9 fusion.108
  82.4 7.4 conditional.16
  89.8 7.2 conditional.17
  97.9 8.4 %conditional.18 = (f32[512,12,64]{0,2,1:T(8,128)}) conditional(s32[]{:T(128)} %bitcast.23, () %tuple.126, (s32[512]{0:T(512)S(1)}, s32[512]{0:T(512)S(1)}, bf16[512,12,64]{0,2,1:T(8,128)(2,1)S(1)}, bf16[512,12,64]{0,2,1:T(8,128)(2,1)}, f32[12,512]{1,0:T(8,128)S(1)}, /*index=5*/bf16[512,12,64]{0,2,1:T(8,128)(2,1)}) %tuple.321), branch_computations={%region_22.23_spmd, %region_23.24_spmd} | conditional | flops 818151424 | bytes 4485128 | solution.py:115
  98.1 8.1 %fusion.21 = f32[512,12,64]{0,2,1:T(8,128)} fusion(bf16[512,12,64]{0,2,1:T(8,128)(2,1)} %get-tuple-element.309, f32[12,512]{1,0:T(8,128)S(1)} %get-tuple-element.308, pred[512,512]{1,0:T(8,128)(4,1)S(1)} %broadcast_compare_fusion.6, bf16[512,12,64]{0,2,1:T(8,128)(2,1)S(1)} %get-tuple-element.306, bf16[512,12,64]{0,2,1:T(8,128)(2,1)} %get-tuple-element.307), kind=kOutput, calls=%fused_computation.42 | convolution fusion | flops 817889280 | bytes 4218880 | tf_op jit(solution)/shard_map/while/body/eval_jaxpr/cond/branch_1_fun/hqk,khd->qhd/dot_general | solution.py:111
  106.2 8.7 %conditional.19 = (f32[512,12,64]{0,2,1:T(8,128)}) conditional(s32[]{:T(128)} %bitcast.22, f32[512,12,64]{0,2,1:T(8,128)} %get-tuple-element.688, (s32[512]{0:T(512)S(1)}, bf16[512,12,64]{0,2,1:T(8,128)(2,1)S(1)}, bf16[512,12,64]{0,2,1:T(8,128)(2,1)S(1)}, f32[12,512]{1,0:T(8,128)S(1)}, bf16[512,12,64]{0,2,1:T(8,128)(2,1)}, ...), branch_computations={%region_24.25_spmd, %region_25.26_spmd} | conditional | flops 818544640 | bytes 6055944 | solution.py:115
  106.6 8.3 %bitcast_add_fusion.1 = f32[512,12,64]{0,2,1:T(8,128)} fusion(f32[512,12,64]{0,2,1:T(8,128)} %get-tuple-element.310, bf16[512,12,64]{0,2,1:T(8,128)(2,1)} %get-tuple-element.315, f32[12,512]{1,0:T(8,128)S(1)} %get-tuple-element.314, pred[512,512]{1,0:T(8,128)(4,1)S(1)} %broadcast_compare_fusion.7, bf16[512,12,64]{0,2,1:T(8,128)(2,1)S(1)} %get-tuple-element.312, ...), kind=kOutput, calls=%fused_computation.50 | convolution fusion | flops 818282496 | bytes 5791744 | tf_op jit(solution)/shard_map/while/body/eval_jaxpr/cond/branch_1_fun/hqk,khd->qhd/dot_general | solution.py:111
  116.4 7.4 conditional.12
  123.8 7.5 conditional.13
  132.1 8.3 %conditional.14 = (f32[512,12,64]{0,2,1:T(8,128)}) conditional(s32[]{:T(128)} %bitcast.14, () %tuple.120, (s32[512]{0:T(512)S(1)}, bf16[512,12,64]{0,2,1:T(8,128)(2,1)S(1)}, bf16[512,12,64]{0,2,1:T(8,128)(2,1)}, f32[12,512]{1,0:T(8,128)S(1)}, bf16[512,12,64]{0,2,1:T(8,128)(2,1)}) %tuple.324), branch_computations={%region_10.11_spmd, %region_11.12_spmd} | conditional | flops 818151424 | bytes 4483080 | solution.py:115
  132.3 8.0 %fusion.6 = f32[512,12,64]{0,2,1:T(8,128)} fusion(bf16[512,12,64]{0,2,1:T(8,128)(2,1)} %get-tuple-element.287, f32[12,512]{1,0:T(8,128)S(1)} %get-tuple-element.286, pred[512,512]{1,0:T(8,128)(4,1)S(1)} %broadcast_compare_fusion.2, bf16[512,12,64]{0,2,1:T(8,128)(2,1)S(1)} %get-tuple-element.284, bf16[512,12,64]{0,2,1:T(8,128)(2,1)} %get-tuple-element.285), kind=kOutput, calls=%fused_computation.15 | convolution fusion | flops 817889280 | bytes 4218880 | tf_op jit(solution)/shard_map/while/body/eval_jaxpr/cond/branch_1_fun/hqk,khd->qhd/dot_general | solution.py:111
  140.4 8.7 %conditional.15 = (f32[512,12,64]{0,2,1:T(8,128)}) conditional(s32[]{:T(128)} %bitcast.13, f32[512,12,64]{0,2,1:T(8,128)} %get-tuple-element.685, (s32[512]{0:T(512)S(1)}, s32[512]{0:T(512)S(1)}, bf16[512,12,64]{0,2,1:T(8,128)(2,1)S(1)}, bf16[512,12,64]{0,2,1:T(8,128)(2,1)S(1)}, f32[12,512]{1,0:T(8,128)S(1)}, ...), branch_computations={%region_12.13_spmd, %region_13.14_spmd} | conditional | flops 818544640 | bytes 6057992 | solution.py:115
  140.8 8.3 %bitcast_add_fusion = f32[512,12,64]{0,2,1:T(8,128)} fusion(f32[512,12,64]{0,2,1:T(8,128)} %get-tuple-element.288, bf16[512,12,64]{0,2,1:T(8,128)(2,1)} %get-tuple-element.294, f32[12,512]{1,0:T(8,128)S(1)} %get-tuple-element.293, pred[512,512]{1,0:T(8,128)(4,1)S(1)} %broadcast_compare_fusion.3, bf16[512,12,64]{0,2,1:T(8,128)(2,1)S(1)} %get-tuple-element.291, ...), kind=kOutput, calls=%fused_computation.23 | convolution fusion | flops 818282496 | bytes 5791744 | tf_op jit(solution)/shard_map/while/body/eval_jaxpr/cond/branch_1_fun/hqk,khd->qhd/dot_general | solution.py:111
  156.9 38.9 %multiply_convert_fusion.4 = (bf16[1024,3072]{1,0:T(8,128)(2,1)}, f32[1024,3072]{1,0:T(8,128)}, f32[1024,3072]{1,0:T(8,128)}) fusion(f32[3072]{0:T(1024)S(1)} %bitcast.209, bf16[768,3072]{1,0:T(8,128)(2,1)} %all-gather.12.cloned.1.call-done, f32[1024,768]{0,1:T(8,128)} %copy-done.9, f32[768]{0:T(1024)S(1)} %get-tuple-element.582, ...), kind=kOutput, calls=%fused_computation.101 | convolution fusion | flops 5043388416 | bytes 39348224 | tf_op jit(solution)/shard_map/dot_general | solution.py:247
  195.8 18.8 %all-gather.14.cloned.1.call-done = bf16[3072,768]{1,0:T(8,128)(2,1)} async-done(((bf16[1536,768]{1,0:T(8,128)(2,1)}), bf16[3072,768]{1,0:T(8,128)(2,1)}) %all-gather.14.cloned.1.call-update) | async-done | bytes 4718608 | tf_op jit(solution)/shard_map/all_gather | solution.py:245
  214.6 17.3 %fusion.112 = (bf16[3072]{0:T(1024)(128)(2,1)}, bf16[1024,3072]{1,0:T(8,128)(2,1)}) fusion(f32[1024,3072]{1,0:T(8,128)} %get-tuple-element.601, bf16[1024,768]{1,0:T(8,128)(2,1)S(1)} %copy-done.24, bf16[3072,768]{1,0:T(8,128)(2,1)} %all-gather.14.cloned.1.call-done, f32[1024,3072]{1,0:T(8,128)} %get-tuple-element.632, f32[3072]{0:T(1024)S(1)} %bitcast.210), kind=kOutput, calls=%fused_computation.202 | convolution fusion | flops 4882166784 | bytes 37767168 | tf_op jit(solution)/shard_map/dot_general | solution.py:259
  232.0 10.7 %fusion.110 = (bf16[768]{0:T(1024)(128)(2,1)}, f32[1024,768]{1,0:T(8,128)}) fusion(bf16[1024,3072]{1,0:T(8,128)(2,1)} %get-tuple-element.638, bf16[768,3072]{1,0:T(8,128)(2,1)} %all-gather.12.cloned.1.call-done), kind=kOutput, calls=%fused_computation.200 | convolution fusion | flops 4832623616 | bytes 14157312 | tf_op jit(solution)/shard_map/dot_general | solution.py:264
  255.6 9.7 %convolution_convert_fusion.1 = bf16[768,3072]{1,0:T(8,128)(2,1)} fusion(bf16[1024,3072]{1,0:T(8,128)(2,1)} %get-tuple-element.638, f32[1024,768]{0,1:T(8,128)S(1)} %copy-done.10, f32[768]{0:T(1024)S(1)} %get-tuple-element.582, f32[768]{0:T(1024)S(1)} %get-tuple-element.580, f32[1024]{0:T(1024)S(1)} %add_rsqrt_fusion, f32[1024]{0:T(1024)S(1)} %broadcast_multiply_fusion.4), kind=kOutput, calls=%fused_computation.116 | convolution fusion | flops 4838129664 | bytes 14170112 | tf_op jit(solution)/shard_map/dot_general | solution.py:262
  266.8 9.7 %convolution_convert_fusion = bf16[3072,768]{1,0:T(8,128)(2,1)} fusion(bf16[1024,3072]{1,0:T(8,128)(2,1)} %get-tuple-element.600, bf16[1024,768]{1,0:T(8,128)(2,1)S(1)} %copy-done.25), kind=kOutput, calls=%fused_computation.115 | convolution fusion | flops 4834197504 | bytes 12582912 | tf_op jit(solution)/shard_map/dot_general | solution.py:261
  283.3 14.5 %conditional.20 = (f32[512,12,64]{0,2,1:T(8,128)}, f32[512,12,64]{0,2,1:T(8,128)S(1)}, f32[512,12,64]{0,2,1:T(8,128)S(1)}) conditional(s32[]{:T(128)} %bitcast.14, () %tuple.132, (s32[512]{0:T(512)S(1)}, bf16[512,12,64]{0,2,1:T(8,128)(2,1)S(1)}, bf16[512,12,64]{0,2,1:T(8,128)(2,1)S(1)}, f32[12,512]{1,0:T(8,128)S(1)}, ...), branch_computations={%region_31.32_spmd.clone, %region_32.33_spmd.clone} | conditional | flops 2045771776 | bytes 74000464 | solution.py:179
  285.5 4.8 multiply_convert_fusion.3
  299.4 17.1 %conditional.21 = (f32[512,12,64]{0,2,1:T(8,128)}, f32[512,12,64]{0,2,1:T(8,128)S(1)}, f32[512,12,64]{0,2,1:T(8,128)}) conditional(s32[]{:T(128)} %bitcast.13, f32[512,12,64]{0,2,1:T(8,128)} %get-tuple-element.394, (s32[512]{0:T(512)S(1)}, s32[512]{0:T(512)S(1)}, bf16[512,12,64]{0,2,1:T(8,128)(2,1)S(1)}, bf16[512,12,64]{0,2,1:T(8,128)(2,1)S(1)}, ...), branch_computations={%region_33.34_spmd, %region_34.35_spmd} | conditional | flops 2046164992 | bytes 78721128 | solution.py:179
  301.7 4.8 multiply_convert_fusion
  306.6 4.6 bitcast_add_fusion.2
  317.7 15.4 %conditional.22 = (f32[512,12,64]{0,2,1:T(8,128)S(1)}, f32[512,12,64]{0,2,1:T(8,128)}, f32[512,12,64]{0,2,1:T(8,128)}) conditional(s32[]{:T(128)} %bitcast.23, (f32[512,12,64]{0,2,1:T(8,128)}, f32[512,12,64]{0,2,1:T(8,128)}) %tuple.297, (s32[512]{0:T(512)S(1)}, s32[512]{0:T(512)S(1)}, bf16[512,12,64]{0,2,1:T(8,128)(2,1)S(1)}, ...), branch_computations={%region_35.36_spmd, %region_36.37_spmd} | conditional | flops 2046558208 | bytes 105459936 | solution.py:179
  320.0 4.8 multiply_convert_fusion.1
  333.1 17.4 %conditional.23 = (f32[512,12,64]{0,2,1:T(8,128)S(1)}, f32[512,12,64]{0,2,1:T(8,128)}, f32[512,12,64]{0,2,1:T(8,128)}) conditional(s32[]{:T(128)} %bitcast.22, (f32[512,12,64]{0,2,1:T(8,128)S(1)}, f32[512,12,64]{0,2,1:T(8,128)}, f32[512,12,64]{0,2,1:T(8,128)}) %tuple.295, (s32[512]{0:T(512)S(1)}, bf16[512,12,64]{0,2,1:T(8,128)(2,1)S(1)}, ...), branch_computations={%region_37.38_spmd, %region_38.39_spmd} | conditional | flops 2046951424 | bytes 91302032 | solution.py:179
  335.6 4.8 multiply_convert_fusion.2
  342.6 5.6 bitcast_add_fusion.6
  358.4 5.9 convolution_convert_fusion.2
  364.9 9.1 %fusion.111 = (bf16[768]{0:T(1024)(128)(2,1)S(1)}, f32[1024,768]{1,0:T(8,128)}) fusion(bf16[768,2304]{1,0:T(8,128)(2,1)} %all-gather.8.cloned.1.call-done, bf16[1024,768]{0,1:T(8,128)(2,1)} %bitcast.167, bf16[1024,768]{0,1:T(8,128)(2,1)} %bitcast.163, bf16[1024,768]{0,1:T(8,128)(2,1)} %bitcast.169), kind=kOutput, calls=%fused_computation.201 | convolution fusion | flops 3638820096 | bytes 11404800 | tf_op jit(solution)/shard_map/dot_general | solution.py:317
  384.8 18.4 %reduce-scatter.23.cloned.1.call-done = bf16[1536,768]{1,0:T(8,128)(2,1)} async-done(((bf16[3072,768]{1,0:T(8,128)(2,1)}), bf16[1536,768]{1,0:T(8,128)(2,1)}) %reduce-scatter.23.cloned.1.call-update) | async-done | bytes 2359312 | tf_op jit(solution)/shard_map/reduce_scatter | solution.py:272
  403.3 50.6 %reduce-scatter.17.cloned.1.call-done = bf16[384,2304]{1,0:T(8,128)(2,1)} async-done(((bf16[768,2304]{1,0:T(8,128)(2,1)}), bf16[384,2304]{1,0:T(8,128)(2,1)}) %reduce-scatter.17.cloned.1.call-update) | async-done | bytes 1769488 | tf_op jit(solution)/shard_map/reduce_scatter | solution.py:331
  455.1 9.1 %add_convert_fusion.1 = bf16[1024,768]{0,1:T(8,128)(2,1)S(1)} fusion(f32[1024,768]{0,1:T(8,128)} %copy-done.9, bf16[1024,3072]{1,0:T(8,128)(2,1)} %get-tuple-element.600, bf16[3072,768]{1,0:T(8,128)(2,1)} %all-gather.14.cloned.1.call-done, f32[768]{0:T(1024)S(1)} %copy-done.66), kind=kOutput, calls=%fused_computation.149 | convolution fusion | flops 4834197504 | bytes 15731712 | tf_op jit(solution)/shard_map/dot_general | solution.py:251
  465.8 5.5 fusion.81
  474.9 5.0 all-reduce
  481.9 11.5 %reduce-scatter.29.cloned.1.call-done = bf16[384,2]{1,0:T(8,128)(2,1)} async-done(((bf16[768,2]{1,0:T(8,128)(2,1)}), bf16[384,2]{1,0:T(8,128)(2,1)}) %reduce-scatter.29.cloned.1.call-update) | async-done | bytes 1552
  494.4 12.1 %reduce-scatter.31.cloned.1.call-done = bf16[384,2]{1,0:T(8,128)(2,1)} async-done(((bf16[768,2]{1,0:T(8,128)(2,1)}), bf16[384,2]{1,0:T(8,128)(2,1)}) %reduce-scatter.31.cloned.1.call-update) | async-done | bytes 1552
  507.5 63.3 %all-reduce.1 = (bf16[2,384]{1,0:T(2,128)(2,1)S(1)}, bf16[2,384]{1,0:T(2,128)(2,1)S(1)}, bf16[2,384]{1,0:T(2,128)(2,1)S(1)}, bf16[2,384]{1,0:T(2,128)(2,1)S(1)}, bf16[1536]{0:T(1024)(128)(2,1)S(1)}) all-reduce(bf16[2,384]{1,0:T(2,128)(2,1)S(1)} %copy.96, ...), channel_id=1, replica_groups=mesh['replica'=16,'shard'=2] {'replica'}, use_global_device_ids=true, to_apply=%region_44.45 | all-reduce | flops 4608 | bytes 18432 | tf_op jit(solution)/shard_map/psum | solution.py:345
  573.7 63.1 %all-reduce.5.cloned.1.call-done = (bf16[384,768]{1,0:T(8,128)(2,1)}, bf16[768,1536]{1,0:T(8,128)(2,1)}, bf16[1536,768]{1,0:T(8,128)(2,1)}) async-done(((bf16[384,768]{1,0:T(8,128)(2,1)}, bf16[768,1536]{1,0:T(8,128)(2,1)}, bf16[1536,768]{1,0:T(8,128)(2,1)}), (bf16[384,768]{1,0:T(8,128)(2,1)}, bf16[768,1536]{1,0:T(8,128)(2,1)}, bf16[1536,768]{1,0:T(8,128)(2,1)})) %all-reduce.5.cloned.1.call-update) | async-done | bytes 5308432 | tf_op jit(solution)/shard_map/psum | solution.py:349
  639.1 4.5 convert_element_type.277
  646.7 135.1 %all-gather.16.cloned.1.call-done = bf16[6144,2304]{1,0:T(8,128)(2,1)} async-done(((bf16[384,2304]{1,0:T(8,128)(2,1)}), bf16[6144,2304]{1,0:T(8,128)(2,1)}) %all-gather.16.cloned.1.call-update) | async-done | bytes 28311568 | tf_op jit(solution)/shard_map/all_gather | solution.py:13
  781.9 10.2 %reduce_sum.227 = bf16[384,2304]{1,0:T(8,128)(2,1)S(1)} reduce(bf16[16,384,2304]{2,1,0:T(8,128)(2,1)} %bitcast.160, bf16[]{:T(256)} %constant.202.clone.1), dimensions={0}, to_apply=%region_50.51 | reduce | flops 13271040 | bytes 30081026 | tf_op jit(solution)/shard_map/reduce_sum | solution.py:14
  (317 shorter events, 161.8 us)
Async XLA Ops:
  7.2 13.9 %copy-start.71 = (bf16[2,384]{1,0:T(2,128)(2,1)S(1)}, bf16[2,384]{1,0:T(2,128)(2,1)}, u32[]{:S(2)}) copy-start(bf16[2,384]{1,0:T(2,128)(2,1)} %param.44) | copy-start | bytes 4612
  7.2 21.5 %copy-start.72 = (bf16[2,384]{1,0:T(2,128)(2,1)S(1)}, bf16[2,384]{1,0:T(2,128)(2,1)}, u32[]{:S(2)}) copy-start(bf16[2,384]{1,0:T(2,128)(2,1)} %param.40) | copy-start | bytes 4612
  7.2 54.7 %all-gather.8.cloned.1.call-start = ((), (), s32[]{:S(2)}) async-start(), calls=%async_computation.8 | async-start | bytes 5308416 | tf_op jit(solution)/shard_map/all_gather | solution.py:217
  7.9 25.2 %copy-start.73 = (bf16[2,384]{1,0:T(2,128)(2,1)S(1)}, bf16[2,384]{1,0:T(2,128)(2,1)}, u32[]{:S(2)}) copy-start(bf16[2,384]{1,0:T(2,128)(2,1)} %param.39) | copy-start | bytes 4612
  8.0 143.4 %all-gather.10.cloned.1.call-start = ((), (), s32[]{:S(2)}) async-start(), calls=%async_computation.9 | async-start | bytes 1769472 | tf_op jit(solution)/shard_map/all_gather | solution.py:219
  8.7 148.2 %all-gather.12.cloned.1.call-start = ((), (), s32[]{:S(2)}) async-start(), calls=%async_computation.10 | async-start | bytes 7077888 | tf_op jit(solution)/shard_map/all_gather | solution.py:243
  9.4 28.8 %copy-start.74 = (bf16[2,384]{1,0:T(2,128)(2,1)S(1)}, bf16[2,384]{1,0:T(2,128)(2,1)}, u32[]{:S(2)}) copy-start(bf16[2,384]{1,0:T(2,128)(2,1)} %param.42) | copy-start | bytes 4612
  9.4 33.2 %copy-start.69 = (bf16[1536]{0:T(1024)(128)(2,1)S(1)}, bf16[1536]{0:T(1024)(128)(2,1)}, u32[]{:S(2)}) copy-start(bf16[1536]{0:T(1024)(128)(2,1)} %param.46) | copy-start | bytes 9220
  9.5 37.7 %copy-start.23 = (bf16[1024,768]{1,0:T(8,128)(2,1)S(1)}, bf16[1024,768]{1,0:T(8,128)(2,1)}, u32[]{:S(2)}) copy-start(bf16[1024,768]{1,0:T(8,128)(2,1)} %param.37) | copy-start | bytes 4718596
  9.5 205.2 %all-gather.14.cloned.1.call-start = ((), (), s32[]{:S(2)}) async-start(), calls=%async_computation.11 | async-start | bytes 7077888 | tf_op jit(solution)/shard_map/all_gather | solution.py:245
  10.0 374.8 %reduce-scatter.19.cloned.1.call-start = ((), (), s32[]{:S(2)}) async-start(), calls=%async_computation.13 | async-start | bytes 1769472 | tf_op jit(solution)/shard_map/reduce_scatter | solution.py:337
  13.3 127.1 %copy-start.49 = (s32[1,512]{1,0:T(1,128)}, s32[1,512]{1,0:T(1,128)S(1)}, u32[]{:S(2)}) copy-start(s32[1,512]{1,0:T(1,128)S(1)} %get-tuple-element.623) | copy-start | bytes 6148
  13.3 127.1 %copy-start.51 = (s32[1,512]{1,0:T(1,128)}, s32[1,512]{1,0:T(1,128)S(1)}, u32[]{:S(2)}) copy-start(s32[1,512]{1,0:T(1,128)S(1)} %get-tuple-element.622) | copy-start | bytes 6148
  28.7 122.6 %copy-start.2 = (bf16[1024,768]{0,1:T(8,128)(2,1)}, bf16[1024,768]{0,1:T(8,128)(2,1)S(1)}, u32[]{:S(2)}) copy-start(bf16[1024,768]{0,1:T(8,128)(2,1)S(1)} %copy.79) | copy-start | bytes 4718596
  33.1 36.7 %copy-start.67 = (f32[768]{0:T(1024)}, f32[768]{0:T(1024)S(1)}, u32[]{:S(2)}) copy-start(f32[768]{0:T(1024)S(1)} %get-tuple-element.583) | copy-start | bytes 9220
  37.5 32.3 %copy-start.55 = (f32[768]{0:T(1024)}, f32[768]{0:T(1024)S(1)}, u32[]{:S(2)}) copy-start(f32[768]{0:T(1024)S(1)} %get-tuple-element.581) | copy-start | bytes 9220
  37.8 32.0 %copy-start.53 = (f32[1024]{0:T(1024)}, f32[1024]{0:T(1024)S(1)}, u32[]{:S(2)}) copy-start(f32[1024]{0:T(1024)S(1)} %broadcast_multiply_fusion.5) | copy-start | bytes 12292
  38.3 31.6 %copy-start.57 = (f32[1024]{0:T(1024)}, f32[1024]{0:T(1024)S(1)}, u32[]{:S(2)}) copy-start(f32[1024]{0:T(1024)S(1)} %add_rsqrt_fusion.1) | copy-start | bytes 12292
  72.2 34.0 %copy-start.4 = (bf16[512,768]{0,1:T(8,128)(2,1)}, bf16[512,768]{0,1:T(8,128)(2,1)S(1)}, u32[]{:S(2)}) copy-start(bf16[512,768]{0,1:T(8,128)(2,1)S(1)} %copy.85) | copy-start | bytes 2359300
  77.5 62.9 %copy-start.6 = (bf16[512,768]{0,1:T(8,128)(2,1)}, bf16[512,768]{0,1:T(8,128)(2,1)S(1)}, u32[]{:S(2)}) copy-start(bf16[512,768]{0,1:T(8,128)(2,1)S(1)} %copy.82) | copy-start | bytes 2359300
  97.9 8.4 %copy-start.59 = (f32[12,512]{1,0:T(8,128)}, f32[12,512]{1,0:T(8,128)S(1)}, u32[]{:S(2)}) copy-start(f32[12,512]{1,0:T(8,128)S(1)} %log_add_fusion) | copy-start | bytes 73732
  116.4 24.0 %copy-start = (bf16[512,768]{0,1:T(8,128)(2,1)}, bf16[512,768]{0,1:T(8,128)(2,1)S(1)}, u32[]{:S(2)}) copy-start(bf16[512,768]{0,1:T(8,128)(2,1)S(1)} %copy.80) | copy-start | bytes 2359300
  132.1 8.3 %copy-start.61 = (f32[12,512]{1,0:T(8,128)}, f32[12,512]{1,0:T(8,128)S(1)}, u32[]{:S(2)}) copy-start(f32[12,512]{1,0:T(8,128)S(1)} %log_add_fusion.1) | copy-start | bytes 73732
  156.9 57.8 %copy-start.24 = (bf16[1024,768]{1,0:T(8,128)(2,1)S(1)}, bf16[1024,768]{1,0:T(8,128)(2,1)}, u32[]{:S(2)}) copy-start(bf16[1024,768]{1,0:T(8,128)(2,1)} %param.37) | copy-start | bytes 4718596
  255.6 129.3 %reduce-scatter.21.cloned.1.call-start = ((), (), s32[]{:S(2)}) async-start(), calls=%async_computation.14 | async-start | bytes 7077888 | tf_op jit(solution)/shard_map/reduce_scatter | solution.py:266
  265.4 137.8 %reduce-scatter.23.cloned.1.call-start = ((), (), s32[]{:S(2)}) async-start(), calls=%async_computation.15 | async-start | bytes 7077888 | tf_op jit(solution)/shard_map/reduce_scatter | solution.py:272
  276.5 177.4 %reduce-scatter.17.cloned.1.call-start = ((), (), s32[]{:S(2)}) async-start(), calls=%async_computation.12 | async-start | bytes 5308416 | tf_op jit(solution)/shard_map/reduce_scatter | solution.py:331
  283.2 14.6 %copy-start.7 = (bf16[512,768]{0,1:T(8,128)(2,1)S(1)}, bf16[512,768]{0,1:T(8,128)(2,1)}, u32[]{:S(2)}) copy-start(bf16[512,768]{0,1:T(8,128)(2,1)} %copy-done.6) | copy-start | bytes 2359300
  283.2 14.6 %copy-start.50 = (s32[1,512]{1,0:T(1,128)S(1)}, s32[1,512]{1,0:T(1,128)}, u32[]{:S(2)}) copy-start(s32[1,512]{1,0:T(1,128)} %copy-done.49) | copy-start | bytes 6148
  297.8 18.7 %copy-start.5 = (bf16[512,768]{0,1:T(8,128)(2,1)S(1)}, bf16[512,768]{0,1:T(8,128)(2,1)}, u32[]{:S(2)}) copy-start(bf16[512,768]{0,1:T(8,128)(2,1)} %copy-done.4) | copy-start | bytes 2359300
  297.8 18.7 %copy-start.60 = (f32[12,512]{1,0:T(8,128)S(1)}, f32[12,512]{1,0:T(8,128)}, u32[]{:S(2)}) copy-start(f32[12,512]{1,0:T(8,128)} %copy-done.59) | copy-start | bytes 73732
  333.1 19.1 %copy-start.15 = (f32[512,12,64]{0,2,1:T(8,128)S(1)}, f32[512,12,64]{0,2,1:T(8,128)}, u32[]{:S(2)}) copy-start(f32[512,12,64]{0,2,1:T(8,128)} %get-tuple-element.403) | copy-start | bytes 4718596
  342.6 5.7 copy-start.17
  354.1 4.3 copy-start.3
  354.1 4.3 copy-start.54
  354.1 4.3 copy-start.56
  354.1 4.3 copy-start.58
  358.4 6.2 copy-start.26
  364.4 115.6 %reduce-scatter.25.cloned.1.call-start = ((), (), s32[]{:S(2)}) async-start(), calls=%async_computation.17 | async-start | bytes 294912
  374.0 7.6 copy-start.70
  380.7 73.2 %copy-start.75 = (u32[32]{0:T(128)S(1)}, u32[32]{0:T(128)}, u32[]{:S(2)}) copy-start(u32[32]{0:T(128)} %constant.210) | copy-start | bytes 388
  380.7 74.4 %copy-start.66 = (f32[768]{0:T(1024)S(1)}, f32[768]{0:T(1024)}, u32[]{:S(2)}) copy-start(f32[768]{0:T(1024)} %get-tuple-element.578) | copy-start | bytes 9220
  381.7 99.2 %reduce-scatter.27.cloned.1.call-start = ((), (), s32[]{:S(2)}) async-start(), calls=%async_computation.18 | async-start | bytes 294912
  382.8 110.6 %reduce-scatter.29.cloned.1.call-start = ((), (), s32[]{:S(2)}) async-start(), calls=%async_computation.19 | async-start | bytes 294912
  383.8 122.7 %reduce-scatter.31.cloned.1.call-start = ((), (), s32[]{:S(2)}) async-start(), calls=%async_computation.20 | async-start | bytes 294912
  384.7 252.1 %all-reduce.5.cloned.1.call-start = ((), (), s32[]{:S(2)}) async-start(), calls=%async_computation.21 | async-start | bytes 10616832 | tf_op jit(solution)/shard_map/psum | solution.py:349
  403.2 378.6 %all-gather.16.cloned.1.call-start = ((), (), s32[]{:S(2)}) async-start(), calls=%async_computation.16 | async-start | bytes 30081024 | tf_op jit(solution)/shard_map/all_gather | solution.py:13
  636.8 6.8 copy-start.32
  (42 other events, 95.7 us)
Sparse Core Ops, SparseCore 0:
  9.6 52.3 all-gather.7
  63.5 22.7 all-gather.9
  87.9 62.6 all-gather.11
  151.9 62.6 all-gather.13
  255.7 21.7 reduce-scatter.18
  280.3 59.9 reduce-scatter.20
  343.2 59.9 reduce-scatter.22
  406.1 47.6 reduce-scatter.16
  456.1 10.9 reduce-scatter.24
  469.1 11.0 reduce-scatter.26
  482.4 10.9 reduce-scatter.28
  495.5 10.9 reduce-scatter.30
  510.6 126.2 all-reduce.4
  638.4 143.4 all-gather.15
